TPU v7x, 256 devices: a whole 4x4x8 slice. The times are simulated.
256 devices in a mesh: section: 4 (over y_lo, core), seq: 16 (over y_hi, z), expert: 4 (over x).
Axes of the slice: x: 4, y: 4 (y_hi: 2, y_lo: 2; y = y_hi * 2 + y_lo), z: 8, core: 2. Of those that a mesh axis runs over, the one named last changes fastest.
Arguments:
- queries: bfloat16 [16, 1536, 4096], P(('section', 'expert'), 'seq'), may hold values from -112 to 112
- dec_state: bfloat16 [16, 1536, 4096], P(('section', 'expert'), 'seq'), may hold values from -6 to 6
- enc_kv: bfloat16 [2, 16, 2560, 1024], P(None, ('section', 'expert'), 'seq'), may hold values from -15 to 15
- band_start: int32 [16, 16], P(('section', 'expert'), 'seq'), may hold values from 0 to 2432, as said below
- norm_gain: float32 [4096], replicated, may hold values from 0.5 to 1.5
- route_ids: int32 [16, 1536, 1], P(('section', 'expert'), 'seq'), may hold values from 0 to 31; in each aligned block of 96 rows (0 to 95, 96 to 191, ..., all dimensions but the last counted through in order) at most 3 rows name the same one
- keep: int32 [16, 1536], P(('section', 'expert'), 'seq'), may hold values 0 or 1
- route_prob: float32 [16, 1536], P(('section', 'expert'), 'seq'), may hold values from 0.25 to 1
- w_in: bfloat16 [32, 5120, 4096], P('seq', ('section', 'expert')), may hold values from -0.09375 to 0.09375
- w_out: bfloat16 [32, 5120, 4096], P('seq', ('section', 'expert')), may hold values from -0.078125 to 0.078125
Outputs:
- mixed: bfloat16 [16, 1536, 4096], P(('section', 'expert'), 'seq')
Inputs may be any that keep to these rules, and one draw needn't show every extreme that they name: `band_start`: block q's band lies within encoder frames (q - 1) * 160 to (q + 2) * 160 - 1. `route_ids`: among the tokens of one device no expert is named more than 3 times.
All inputs are finite; a program needn't handle non-finite values. No bound on the sum of `keep` on one device may be relied on, other than what follows from the above.
Results may differ from a plain program's by a relative error of at most 0.011.
Values may be sent and summed in bfloat16 or wider, within the bound.
A program may use at most 128 MiB of HBM per device.

v0:
```python
import math
import jax
import jax.numpy as jnp
from jax import lax
from jax.sharding import PartitionSpec as P

D = 4096
HEADS = 32
KV_HEADS = 8
DH = 128
WIN = 128


def shifted(block, axis, distance):
    devices = range(lax.axis_size(axis))
    route = [((i - distance) % len(devices), i) for i in devices]
    return lax.ppermute(block, axis, route)


def extended(cells, sides, width):
    for axis, dim in sides:
        count = lax.axis_size(axis)
        ends = count - 1
        head = lax.slice_in_dim(cells, 0, width, axis=dim)
        tail = lax.slice_in_dim(cells, cells.shape[dim] - width, cells.shape[dim], axis=dim)
        cells = jnp.concatenate(
            [
                lax.ppermute(tail, axis, [(i, (i + 1) % count) for i in range(ends)]),
                cells,
                lax.ppermute(head, axis, [((i + 1) % count, i) for i in range(ends)]),
            ],
            axis=dim,
        )
    return cells


def cross_attend(query_rows, band_pair):
    tok_count = query_rows.shape[0]
    groups = HEADS // KV_HEADS
    grouped = query_rows.reshape(tok_count, KV_HEADS, groups, DH)
    keys_b = band_pair[0].reshape(WIN, KV_HEADS, DH)
    values_b = band_pair[1].reshape(WIN, KV_HEADS, DH)
    scores = jnp.einsum(
        "tkgd,wkd->kgtw", grouped, keys_b, preferred_element_type=jnp.float32
    ) / math.sqrt(DH)
    row_peak = jnp.max(scores, axis=-1, keepdims=True)
    weights = jnp.exp(scores - row_peak)
    row_total = jnp.sum(weights, axis=-1)
    rounded = weights.astype(jnp.bfloat16)
    context = jnp.einsum("kgtw,wkd->tkgd", rounded, values_b, preferred_element_type=jnp.float32)
    context = context / jnp.transpose(row_total, (2, 0, 1))[..., None]
    return context.reshape(tok_count, HEADS * DH)


def body(
    queries, dec_state, enc_kv, band_start, norm_gain, route_ids, keep, route_prob, w_in, w_out
):
    own_pair = shifted(enc_kv[:, 0], "section", 1)
    frames_dev = own_pair.shape[1]
    offset = band_start[0, 0]
    position = lax.axis_index("seq")
    widened = extended(own_pair, (("seq", 1),), frames_dev)
    local_first = offset - (position - 1) * frames_dev
    band_pair = lax.dynamic_slice_in_dim(widened, local_first, WIN, 1)
    context = cross_attend(queries[0], band_pair)
    state = dec_state[0].astype(jnp.float32) + context
    normed = (
        state * lax.rsqrt(jnp.mean(state * state, axis=-1, keepdims=True) + 1e-06) * norm_gain
    ).astype(jnp.bfloat16)
    experts_of = route_ids[0, :, 0]
    tok_count = experts_of.shape[0]
    seq_count = lax.axis_size("seq")
    per_device = w_in.shape[0]
    expert_count = per_device * seq_count
    capacity = max(2, tok_count // expert_count)
    one_hot = (experts_of[:, None] == jnp.arange(expert_count, dtype=jnp.int32)[None, :]).astype(
        jnp.int32
    )
    earlier = jnp.cumsum(one_hot, axis=0) - one_hot
    slot_of = jnp.sum(earlier * one_hot, axis=1)
    target = experts_of * capacity + slot_of
    kept = keep[0] == 1
    slot_ids = jnp.arange(expert_count * capacity, dtype=jnp.int32)
    dispatch = ((slot_ids[:, None] == target[None, :]) & kept[None, :]).astype(jnp.bfloat16)
    outgoing = jnp.dot(dispatch, normed, preferred_element_type=jnp.float32).astype(jnp.bfloat16)
    outgoing = outgoing.reshape(seq_count, per_device, capacity, D)
    arrived = lax.all_to_all(outgoing, "seq", split_axis=0, concat_axis=2, tiled=True)[0]
    hidden = jnp.einsum(
        "emd,efd->emf",
        lax.all_gather(arrived, ("section", "expert"), axis=1, tiled=True),
        w_in,
        preferred_element_type=jnp.float32,
    )
    hidden = jnp.maximum(hidden, 0.0).astype(jnp.bfloat16)
    partials = jnp.einsum("emf,efd->emd", hidden, w_out, preferred_element_type=jnp.float32)
    summed = lax.psum_scatter(
        partials.astype(jnp.bfloat16), ("section", "expert"), scatter_dimension=1, tiled=True
    )
    returned = lax.all_to_all(summed, "seq", split_axis=1, concat_axis=0, tiled=True).reshape(
        expert_count * capacity, D
    )
    expert_out = jnp.einsum("st,sd->td", dispatch, returned, preferred_element_type=jnp.float32)
    scale = (keep[0].astype(jnp.float32) * route_prob[0])[:, None]
    return (state + scale * expert_out).astype(jnp.bfloat16)[None]


def solution(mesh):
    return jax.shard_map(
        body,
        mesh=mesh,
        in_specs=(
            P(("section", "expert"), "seq", None),
            P(("section", "expert"), "seq", None),
            P(None, ("section", "expert"), "seq", None),
            P(("section", "expert"), "seq"),
            P(),
            P(("section", "expert"), "seq", None),
            P(("section", "expert"), "seq"),
            P(("section", "expert"), "seq"),
            P("seq", ("section", "expert"), None),
            P("seq", ("section", "expert"), None),
        ),
        out_specs=P(("section", "expert"), "seq", None),
        check_vma=False,
    )
```

profile of v0, /device:TPU:32, one launch (start us, length us, event | category | flops | bytes accessed | tf_op | source)
XLA Modules:
  0.0 386.1 jit_solution(8837927128330509526)
XLA Ops:
  6.5 10.2 %collective-permute-done = bf16[2,160,1024]{2,1,0:T(8,128)(2,1)S(1)} collective-permute-done((bf16[2,160,1024]{2,1,0:T(8,128)(2,1)}, bf16[2,160,1024]{2,1,0:T(8,128)(2,1)S(1)}, u32[]{:S(2)}, u32[]{:S(2)}) %collective-permute-start) | collective-permute-done | bytes 655392 | tf_op jit(solution)/shard_map/ppermute | solution.py:17
  16.8 3.8 collective-permute-start.1
  20.6 2.8 collective-permute-start.2
  24.8 3.0 reshape_squeeze.11
  27.8 2.3 reshape.52
  31.0 3.7 collective-permute-done.1
  36.1 2.3 collective-permute-done.2
  38.4 2.2 copy.23
  40.6 2.1 fusion.19
  44.7 2.2 fusion.9
  46.9 2.2 copy.27
  49.1 1.9 reshape.48
  52.4 1.5 reshape.49
  54.9 31.5 %all_to_all.30 = bf16[16,2,3,4096]{3,1,2,0:T(2,128)(2,1)} all-to-all(bf16[16,2,3,4096]{3,1,2,0:T(2,128)(2,1)S(1)} %copy.29), channel_id=1, replica_groups=mesh['section'=4,'seq'=16,'expert'=4] {'seq'}, dimensions={0} | all-to-all | bytes 1572864 | tf_op jit(solution)/shard_map/all_to_all | solution.py:87
  86.7 73.5 %all-gather.2.cloned.1.call-done = bf16[2,768,4096]{2,0,1:T(2,128)(2,1)} async-done(((bf16[2,48,4096]{2,0,1:T(2,128)(2,1)}), bf16[2,768,4096]{2,0,1:T(2,128)(2,1)}) %all-gather.2.cloned.1.call-update) | async-done | bytes 12582928 | tf_op jit(solution)/shard_map/all_gather | solution.py:90
  160.2 22.0 %maximum_convert_fusion = bf16[2,768,320]{1,2,0:T(8,128)(2,1)S(1)} fusion(bf16[2,320,4096]{2,1,0:T(8,128)(2,1)} %param.18, bf16[2,768,4096]{2,0,1:T(2,128)(2,1)} %all-gather.2.cloned.1.call-done), kind=kOutput, calls=%fused_computation.11 | convolution fusion | flops 4027514880 | bytes 18808832 | tf_op jit(solution)/shard_map/emd,efd->emf/dot_general | solution.py:88
  182.2 12.1 %convolution_convert_fusion = bf16[2,768,4096]{2,1,0:T(8,128)(2,1)} fusion(bf16[2,768,320]{1,2,0:T(8,128)(2,1)S(1)} %maximum_convert_fusion, bf16[2,320,4096]{2,1,0:T(8,128)(2,1)} %param.19), kind=kOutput, calls=%fused_computation.2 | convolution fusion | flops 4032823296 | bytes 18808832 | tf_op jit(solution)/shard_map/emf,efd->emd/dot_general | solution.py:95
  194.4 143.6 %reduce-scatter.2.cloned.1.call-done = bf16[2,48,4096]{2,1,0:T(8,128)(2,1)} async-done(((bf16[2,768,4096]{2,1,0:T(8,128)(2,1)}), bf16[2,48,4096]{2,1,0:T(8,128)(2,1)}) %reduce-scatter.2.cloned.1.call-update) | async-done | bytes 786448 | tf_op jit(solution)/shard_map/reduce_scatter | solution.py:96
  338.0 2.8 copy.31
  340.8 9.7 %all-to-all-start.1 = ((bf16[2,48,4096]{2,0,1:T(2,128)(2,1)}), bf16[2,48,4096]{2,0,1:T(2,128)(2,1)S(1)}, u32[]{:S(2)}, u32[]{:S(2)}) async-start(bf16[2,48,4096]{2,0,1:T(2,128)(2,1)} %copy.31), calls=%async_computation.2 | async-start | bytes 1572864 | tf_op jit(solution)/shard_map/all_to_all | solution.py:99
  350.5 22.1 %all-to-all-done.1 = bf16[2,48,4096]{2,0,1:T(2,128)(2,1)S(1)} async-done(((bf16[2,48,4096]{2,0,1:T(2,128)(2,1)}), bf16[2,48,4096]{2,0,1:T(2,128)(2,1)S(1)}, u32[]{:S(2)}, u32[]{:S(2)}) %all-to-all-start.1) | async-done | bytes 786464 | tf_op jit(solution)/shard_map/all_to_all | solution.py:99
  373.5 1.8 copy.32
  375.3 1.4 reshape.50
  376.7 2.5 fusion.4
  (35 shorter events, 8.4 us)
Async XLA Ops:
  6.5 21.3 %copy-start = (bf16[1,96,4096]{2,1,0:T(8,128)(2,1)S(1)}, bf16[1,96,4096]{2,1,0:T(8,128)(2,1)}, u32[]{:S(2)}) copy-start(bf16[1,96,4096]{2,1,0:T(8,128)(2,1)} %param.11) | copy-start | bytes 2359300
  6.5 153.6 %all-gather.2.cloned.1.call-start = ((), (), s32[]{:S(2)}) async-start(), calls=%async_computation.3 | async-start | bytes 13369344 | tf_op jit(solution)/shard_map/all_gather | solution.py:90
  6.5 10.2 %collective-permute-start = (bf16[2,160,1024]{2,1,0:T(8,128)(2,1)}, bf16[2,160,1024]{2,1,0:T(8,128)(2,1)S(1)}, u32[]{:S(2)}, u32[]{:S(2)}) collective-permute-start(bf16[2,160,1024]{2,1,0:T(8,128)(2,1)} %bitcast.64), channel_id=1, source_target_pairs={{192,0},{0,64},{64,128},{128,192},{193,1},{1,65},{65,129},{129,193... | collective-permute-start | bytes 1966088 | tf_op jit(solution)/shard_map/ppermute | solution.py:17
  16.8 17.9 %collective-permute-start.1 = (bf16[2,160,1024]{2,1,0:T(8,128)(2,1)S(1)}, bf16[2,160,1024]{2,1,0:T(8,128)(2,1)}, u32[]{:S(2)}, u32[]{:S(2)}) collective-permute-start(bf16[2,160,1024]{2,1,0:T(8,128)(2,1)S(1)} %collective-permute-done), channel_id=1, source_target_pairs={{0,4},{4,8},{8,12},{12,16},{16,20},{20,24},{24,28},{28,32},{32,36}... | collective-permute-start | bytes 1966088 | tf_op jit(solution)/shard_map/ppermute | solution.py:28
  20.6 17.9 %collective-permute-start.2 = (bf16[2,160,1024]{2,1,0:T(8,128)(2,1)S(1)}, bf16[2,160,1024]{2,1,0:T(8,128)(2,1)}, u32[]{:S(2)}, u32[]{:S(2)}) collective-permute-start(bf16[2,160,1024]{2,1,0:T(8,128)(2,1)S(1)} %collective-permute-done), channel_id=1, source_target_pairs={{4,0},{8,4},{12,8},{16,12},{20,16},{24,20},{28,24},{32,28},{36,32}... | collective-permute-start | bytes 1966088 | tf_op jit(solution)/shard_map/ppermute | solution.py:30
  27.8 2.5 copy-start.5
  27.8 2.7 copy-start.6
  40.6 2.2 copy-start.2
  42.8 1.9 copy-start.3
  49.1 1.9 copy-start.4
  86.4 251.5 %reduce-scatter.2.cloned.1.call-start = ((), (), s32[]{:S(2)}) async-start(), calls=%async_computation.4 | async-start | bytes 13369344 | tf_op jit(solution)/shard_map/reduce_scatter | solution.py:96
  194.4 156.1 %copy-start.7 = (f32[1,96]{1,0:T(1,128)S(1)}, f32[1,96]{1,0:T(1,128)}, u32[]{:S(2)}) copy-start(f32[1,96]{1,0:T(1,128)} %param.17) | copy-start | bytes 1156
  340.8 31.8 %all-to-all-start.1 = ((bf16[2,48,4096]{2,0,1:T(2,128)(2,1)}), bf16[2,48,4096]{2,0,1:T(2,128)(2,1)S(1)}, u32[]{:S(2)}, u32[]{:S(2)}) async-start(bf16[2,48,4096]{2,0,1:T(2,128)(2,1)} %copy.31), calls=%async_computation.2 | async-start | bytes 1572864 | tf_op jit(solution)/shard_map/all_to_all | solution.py:99
  372.6 0.9 copy-start.1
Sparse Core Ops, SparseCore 0:
  86.6 73.5 all-gather.1
  194.5 143.4 reduce-scatter.1
where the time goes:
time: 387 us; the launch traced here: 386 us
  waiting for transfers between devices  255 us (66%)
  matrix products  41 us (11%)
  blocking collectives  31.5 us (8%)
  local copies, waits for them, and re-layouts  23 us (6%)
  starting transfers between devices  16.5 us (4%)
  between operations  14.2 us (4%)
  other arithmetic  4.26 us (1%)
    reduce_scatter x1, waiting for transfers between devices, body(): lax.psum_scatter(partials.astype(jnp.bfloat16), ('section', 'expert'), sc...  144 us
    all_gather x1, waiting for transfers between devices, body(): lax.all_gather(arrived, ('section', 'expert'), axis=1, tiled=True)  73.5 us
    all_to_all x1, blocking collectives, body(): lax.all_to_all(outgoing, 'seq', split_axis=0, concat_axis=2, tiled=True)[0]  31.5 us
    all_to_all x1, waiting for transfers between devices, body(): lax.all_to_all(summed, 'seq', split_axis=1, concat_axis=0, tiled=True)  22.1 us
    dot_general x1, matrix products, body(): jnp.einsum('emd,efd->emf', lax.all_gather(arrived, ('section', 'expert'),...  22 us
    dot_general x1, matrix products, body(): jnp.einsum('emf,efd->emd', hidden, w_out, preferred_element_type=jnp.floa...  12.1 us
    ppermute x1, waiting for transfers between devices, shifted(): return lax.ppermute(block, axis, route)  10.2 us
    all_to_all x1, starting transfers between devices, body(): lax.all_to_all(summed, 'seq', split_axis=1, concat_axis=0, tiled=True)  9.65 us
  transfers between devices with their start and end apart: 6, of which 6 were waited for; matrix products, arithmetic and copies ran while one was open for 2% of the time, Pallas kernels for 0%

commit v1 on v0

--- a/solution.py
+++ b/solution.py
@@ -87,7 +87,15 @@
     arrived = lax.all_to_all(outgoing, "seq", split_axis=0, concat_axis=2, tiled=True)[0]
     hidden = jnp.einsum(
         "emd,efd->emf",
-        lax.all_gather(arrived, ("section", "expert"), axis=1, tiled=True),
+        jnp.concatenate(
+            lax.all_to_all(
+                jnp.stack([arrived] * lax.axis_size(("section", "expert"))),
+                ("section", "expert"),
+                0,
+                0,
+            ),
+            axis=1,
+        ),
         w_in,
         preferred_element_type=jnp.float32,
     )

time: 387 us -> 452 us (1.17)
  blocking collectives: 31.5 us -> 177 us
  waiting for transfers between devices: 255 us -> 175 us
  local copies, waits for them, and re-layouts: 23 us -> 34.7 us
  matrix products: 41 us -> 29.3 us
    all_to_all x0 -> x1, blocking collectives: none -> 146 us  [body(): lax.all_to_all(jnp.stack([arrived] * lax.axis_size(('section', 'expert'))...]
    all_gather x1 -> x0, waiting for transfers between devices: 73.5 us -> none  [body(): lax.all_gather(arrived, ('section', 'expert'), axis=1, tiled=True)]
    dot_general x1, matrix products: 22 us -> 10.3 us  [body(): jnp.einsum('emd,efd->emf', jnp.concatenate(lax.all_to_all(jnp.stack([arri...]
    reduce_scatter x1, waiting for transfers between devices: 144 us -> 137 us  [body(): lax.psum_scatter(partials.astype(jnp.bfloat16), ('section', 'expert'), sc...]
    another operation x0 -> x1, local copies, waits for them, and re-layouts: none -> 6.15 us  [body(): jnp.stack([arrived] * lax.axis_size(('section', 'expert')))]
    all_to_all x0 -> x2, local copies, waits for them, and re-layouts: none -> 5.55 us  [the longest x1 5.11 us: body(): lax.all_to_all(jnp.stack([arrived] * lax.axis_size(('section', 'expert'))...]
  transfers between devices with their start and end apart: 6 -> 5, of which waited for: 6 -> 5; matrix products, arithmetic and copies ran while one was open for 2% -> 2% of each run, Pallas kernels for 0% -> 0%
where the time goes in v1:
time: 452 us; the launch traced here: 451 us
  blocking collectives  177 us (39%)
  waiting for transfers between devices  175 us (39%)
  local copies, waits for them, and re-layouts  34.7 us (8%)
  matrix products  29.3 us (6%)
  starting transfers between devices  16.3 us (4%)
  between operations  14.2 us (3%)
    all_to_all x1, blocking collectives, body(): lax.all_to_all(jnp.stack([arrived] * lax.axis_size(('section', 'expert'))...  146 us
    reduce_scatter x1, waiting for transfers between devices, body(): lax.psum_scatter(partials.astype(jnp.bfloat16), ('section', 'expert'), sc...  137 us
    all_to_all x1, blocking collectives, body(): lax.all_to_all(outgoing, 'seq', split_axis=0, concat_axis=2, tiled=True)[0]  31.4 us
    all_to_all x1, waiting for transfers between devices, body(): lax.all_to_all(summed, 'seq', split_axis=1, concat_axis=0, tiled=True)  22.1 us
    dot_general x1, matrix products, body(): jnp.einsum('emf,efd->emd', hidden, w_out, preferred_element_type=jnp.floa...  12.1 us
    dot_general x1, matrix products, body(): jnp.einsum('emd,efd->emf', jnp.concatenate(lax.all_to_all(jnp.stack([arri...  10.3 us
    ppermute x1, waiting for transfers between devices, shifted(): return lax.ppermute(block, axis, route)  10.2 us
    all_to_all x1, starting transfers between devices, body(): lax.all_to_all(summed, 'seq', split_axis=1, concat_axis=0, tiled=True)  9.64 us
  transfers between devices with their start and end apart: 5, of which 5 were waited for; matrix products, arithmetic and copies ran while one was open for 2% of the time, Pallas kernels for 0%

profile of v1, /device:TPU:32, one launch (start us, length us, event | category | flops | bytes accessed | tf_op | source)
XLA Modules:
  0.0 451.1 jit_solution(10085398648638291218)
XLA Ops:
  6.5 10.2 %collective-permute-done = bf16[2,160,1024]{2,1,0:T(8,128)(2,1)S(1)} collective-permute-done((bf16[2,160,1024]{2,1,0:T(8,128)(2,1)}, bf16[2,160,1024]{2,1,0:T(8,128)(2,1)S(1)}, u32[]{:S(2)}, u32[]{:S(2)}) %collective-permute-start) | collective-permute-done | bytes 655392 | tf_op jit(solution)/shard_map/ppermute | solution.py:17
  16.8 3.8 collective-permute-start.1
  20.6 2.8 collective-permute-start.2
  24.8 3.0 reshape_squeeze.11
  27.8 2.3 reshape.61
  31.0 3.7 collective-permute-done.1
  36.1 2.3 collective-permute-done.2
  38.4 2.2 copy.24
  40.6 2.1 fusion.15
  44.7 2.2 fusion.5
  46.9 2.2 copy.28
  49.1 1.9 reshape.55
  54.9 31.4 %all_to_all.38 = bf16[16,2,3,4096]{3,1,2,0:T(2,128)(2,1)S(1)} all-to-all(bf16[16,2,3,4096]{3,1,2,0:T(2,128)(2,1)S(1)} %copy.30), channel_id=1, replica_groups=mesh['section'=4,'seq'=16,'expert'=4] {'seq'}, dimensions={0} | all-to-all | bytes 1572864 | tf_op jit(solution)/shard_map/all_to_all | solution.py:87
  86.7 6.2 %stack.3 = bf16[16,2,48,4096]{3,2,1,0:T(8,128)(2,1)} broadcast(bf16[2,48,4096]{2,1,0:T(8,128)(2,1)S(1)} %copy.31), dimensions={1,2,3} | broadcast | bytes 13369344 | tf_op jit(solution)/shard_map/stack | solution.py:92
  92.9 145.5 %all_to_all.39 = bf16[16,2,48,4096]{3,2,1,0:T(8,128)(2,1)S(1)} all-to-all(bf16[16,2,48,4096]{3,2,1,0:T(8,128)(2,1)} %stack.3), channel_id=1, replica_groups=mesh['section'=4,'seq'=16,'expert'=4] {'section','expert'}, dimensions={0} | all-to-all | bytes 25165824 | tf_op jit(solution)/shard_map/all_to_all | solution.py:91
  238.4 5.1 %copy.32 = bf16[16,2,48,4096]{3,2,0,1:T(8,128)(2,1)} copy(bf16[16,2,48,4096]{3,2,1,0:T(8,128)(2,1)S(1)} %all_to_all.39) | data formatting | bytes 25165824 | tf_op jit(solution)/shard_map/all_to_all | solution.py:91
  243.5 10.3 %maximum_convert_fusion = bf16[2,768,320]{1,2,0:T(8,128)(2,1)S(1)} fusion(bf16[2,768,4096]{2,1,0:T(8,128)(2,1)} %bitcast.61, bf16[2,320,4096]{2,1,0:T(8,128)(2,1)} %param.18), kind=kOutput, calls=%fused_computation.9 | convolution fusion | flops 4027514880 | bytes 18808832 | tf_op jit(solution)/shard_map/emd,efd->emf/dot_general | solution.py:88
  253.8 12.1 %convolution_convert_fusion = bf16[2,768,4096]{2,1,0:T(8,128)(2,1)} fusion(bf16[2,768,320]{1,2,0:T(8,128)(2,1)S(1)} %maximum_convert_fusion, bf16[2,320,4096]{2,1,0:T(8,128)(2,1)} %param.19), kind=kOutput, calls=%fused_computation | convolution fusion | flops 4032823296 | bytes 18808832 | tf_op jit(solution)/shard_map/emf,efd->emd/dot_general | solution.py:103
  266.0 137.0 %reduce-scatter.2.cloned.1.call-done = bf16[2,48,4096]{2,1,0:T(8,128)(2,1)} async-done(((bf16[2,768,4096]{2,1,0:T(8,128)(2,1)}), bf16[2,48,4096]{2,1,0:T(8,128)(2,1)}) %reduce-scatter.2.cloned.1.call-update) | async-done | bytes 786448 | tf_op jit(solution)/shard_map/reduce_scatter | solution.py:104
  403.0 2.8 copy.33
  405.8 9.6 %all-to-all-start.2 = ((bf16[2,48,4096]{2,0,1:T(2,128)(2,1)}), bf16[2,48,4096]{2,0,1:T(2,128)(2,1)S(1)}, u32[]{:S(2)}, u32[]{:S(2)}) async-start(bf16[2,48,4096]{2,0,1:T(2,128)(2,1)} %copy.33), calls=%async_computation.3 | async-start | bytes 1572864 | tf_op jit(solution)/shard_map/all_to_all | solution.py:107
  415.5 22.1 %all-to-all-done.2 = bf16[2,48,4096]{2,0,1:T(2,128)(2,1)S(1)} async-done(((bf16[2,48,4096]{2,0,1:T(2,128)(2,1)}), bf16[2,48,4096]{2,0,1:T(2,128)(2,1)S(1)}, u32[]{:S(2)}, u32[]{:S(2)}) %all-to-all-start.2) | async-done | bytes 786464 | tf_op jit(solution)/shard_map/all_to_all | solution.py:107
  438.5 1.8 copy.34
  441.7 2.5 fusion.2
  (36 shorter events, 11.5 us)
Async XLA Ops:
  6.5 21.3 %copy-start = (bf16[1,96,4096]{2,1,0:T(8,128)(2,1)S(1)}, bf16[1,96,4096]{2,1,0:T(8,128)(2,1)}, u32[]{:S(2)}) copy-start(bf16[1,96,4096]{2,1,0:T(8,128)(2,1)} %param.11) | copy-start | bytes 2359300
  6.5 396.5 %reduce-scatter.2.cloned.1.call-start = ((), (), s32[]{:S(2)}) async-start(), calls=%async_computation.4 | async-start | bytes 13369344 | tf_op jit(solution)/shard_map/reduce_scatter | solution.py:104
  6.5 10.2 %collective-permute-start = (bf16[2,160,1024]{2,1,0:T(8,128)(2,1)}, bf16[2,160,1024]{2,1,0:T(8,128)(2,1)S(1)}, u32[]{:S(2)}, u32[]{:S(2)}) collective-permute-start(bf16[2,160,1024]{2,1,0:T(8,128)(2,1)} %bitcast.69), channel_id=1, source_target_pairs={{192,0},{0,64},{64,128},{128,192},{193,1},{1,65},{65,129},{129,193... | collective-permute-start | bytes 1966088 | tf_op jit(solution)/shard_map/ppermute | solution.py:17
  16.8 17.9 %collective-permute-start.1 = (bf16[2,160,1024]{2,1,0:T(8,128)(2,1)S(1)}, bf16[2,160,1024]{2,1,0:T(8,128)(2,1)}, u32[]{:S(2)}, u32[]{:S(2)}) collective-permute-start(bf16[2,160,1024]{2,1,0:T(8,128)(2,1)S(1)} %collective-permute-done), channel_id=1, source_target_pairs={{0,4},{4,8},{8,12},{12,16},{16,20},{20,24},{24,28},{28,32},{32,36}... | collective-permute-start | bytes 1966088 | tf_op jit(solution)/shard_map/ppermute | solution.py:28
  20.6 17.9 %collective-permute-start.2 = (bf16[2,160,1024]{2,1,0:T(8,128)(2,1)S(1)}, bf16[2,160,1024]{2,1,0:T(8,128)(2,1)}, u32[]{:S(2)}, u32[]{:S(2)}) collective-permute-start(bf16[2,160,1024]{2,1,0:T(8,128)(2,1)S(1)} %collective-permute-done), channel_id=1, source_target_pairs={{4,0},{8,4},{12,8},{16,12},{20,16},{24,20},{28,24},{32,28},{36,32}... | collective-permute-start | bytes 1966088 | tf_op jit(solution)/shard_map/ppermute | solution.py:30
  27.8 2.5 copy-start.5
  27.8 2.6 copy-start.6
  40.6 2.2 copy-start.2
  42.8 1.9 copy-start.3
  49.1 1.9 copy-start.4
  266.0 149.5 %copy-start.7 = (f32[1,96]{1,0:T(1,128)S(1)}, f32[1,96]{1,0:T(1,128)}, u32[]{:S(2)}) copy-start(f32[1,96]{1,0:T(1,128)} %param.17) | copy-start | bytes 1156
  405.8 31.8 %all-to-all-start.2 = ((bf16[2,48,4096]{2,0,1:T(2,128)(2,1)}), bf16[2,48,4096]{2,0,1:T(2,128)(2,1)S(1)}, u32[]{:S(2)}, u32[]{:S(2)}) async-start(bf16[2,48,4096]{2,0,1:T(2,128)(2,1)} %copy.33), calls=%async_computation.3 | async-start | bytes 1572864 | tf_op jit(solution)/shard_map/all_to_all | solution.py:107
  437.6 0.9 copy-start.1
Sparse Core Ops, SparseCore 0:
  266.1 136.8 reduce-scatter.1
